TPU v7x, 32 devices: a whole 2x2x4 slice. The times are simulated.
32 devices in a mesh: section: 4 (over z), dp: 4 (over y, x), hid: 2 (over core).
Axes of the slice: x: 2, y: 2, z: 4, core: 2. Of those that a mesh axis runs over, the one named last changes fastest.
Arguments:
- forward_input: bfloat16 [4, 768, 2048], P('section', 'dp'), may hold values from -6 to 6
- backward_input: bfloat16 [4, 768, 2048], P('section', 'dp'), may hold values from -6 to 6
- output_grad: bfloat16 [4, 768, 2048], P('section', 'dp'), may hold values from -8 to 8
- norm_gain: float32 [4, 2048], P('section'), may hold values from 0.5 to 1.5
- in_weight: float32 [4, 2, 2048, 512], P('section', None, 'dp', 'hid'), may hold values from -0.125 to 0.125
- out_weight: float32 [4, 512, 2048], P('section', 'hid', 'dp'), may hold values from -0.25 to 0.25
- in_codes: int32 [4, 2, 2048, 512], P('section', None, 'dp', 'hid'), may hold values from 0 to 32511
- out_codes: int32 [4, 512, 2048], P('section', 'hid', 'dp'), may hold values from 0 to 32511
- in_scales: float32 [4, 2, 2, 2048, 2], P('section', None, None, 'dp', 'hid'), may hold values from 0.005 to 0.05
- out_scales: float32 [4, 2, 2, 2048], P('section', None, 'hid', 'dp'), may hold values from 0.005 to 0.05
- section_lags: int32 [4], P('section'), may hold values from 1 to 4
Outputs:
- next_input: bfloat16 [4, 768, 2048], P('section', 'dp')
- input_grad: bfloat16 [4, 768, 2048], P('section', 'dp')
- in_update: float32 [4, 2, 2048, 512], P('section', None, 'dp', 'hid')
- out_update: float32 [4, 512, 2048], P('section', 'hid', 'dp')
Inputs may be any that keep to these rules, and one draw needn't show every extreme that they name: `in_codes`: each code holds a first-moment code of 0 to 126 times 256 plus a second-moment code of 0 to 255. `out_codes`: each code holds a first-moment code of 0 to 126 times 256 plus a second-moment code of 0 to 255.
All inputs are finite; a program needn't handle non-finite values.
Results may differ from a plain program's by a relative error of at most 0.012.
Values may be sent and summed in bfloat16 or wider, within the bound.
A program may use at most 64 MiB of HBM per device.

v0:
```python
import jax
import jax.numpy as jnp
from jax import lax
from jax.sharding import PartitionSpec as P

QB = 256
STEP = 1000


BETA_ONE = 0.9
BETA_TWO = 0.999
ADAM_EPS = 1e-08
NORM_EPS = 1e-06
LEARN_RATE = 0.003


def passed_along(block, axis, distance):
    devices = range(lax.axis_size(axis))
    route = [(i - distance, i) for i in devices if i - distance in devices]
    return lax.ppermute(block, axis, route)


def dequant(codes, first_scale, second_scale):
    high = (codes // 256).astype(jnp.float32)
    low = (codes % 256).astype(jnp.float32)
    moment_m = first_scale * (high - 63.0) / 63.0
    moment_v = jnp.square(second_scale * (0.25 + 0.75 * low / 255.0))
    return (moment_m, moment_v)


def direction(moment_m, moment_v, count):
    return (
        moment_m
        / (1.0 - BETA_ONE**count)
        / (jnp.sqrt(moment_v / (1.0 - BETA_TWO**count)) + ADAM_EPS)
    )


def normalize(inputs, gain):
    values = inputs.astype(jnp.float32)
    factor = lax.rsqrt(jnp.mean(values * values, axis=-1, keepdims=True) + NORM_EPS)
    return ((values * factor * gain).astype(jnp.bfloat16), factor, values)


def local(
    forward_input,
    backward_input,
    output_grad,
    norm_gain,
    in_weight,
    out_weight,
    in_codes,
    out_codes,
    in_scales,
    out_scales,
    section_lags,
):
    lag_value = section_lags[0].astype(jnp.float32)
    gain = norm_gain[0]
    m_in, v_in = dequant(
        in_codes[0],
        jnp.repeat(in_scales[0, 0], QB, axis=-1),
        jnp.repeat(in_scales[0, 1], QB, axis=-1),
    )
    m_out, v_out = dequant(
        out_codes[0],
        jnp.repeat(out_scales[0, 0], QB, axis=0),
        jnp.repeat(out_scales[0, 1], QB, axis=0),
    )
    pred_in = (in_weight[0] - LEARN_RATE * lag_value * direction(m_in, v_in, STEP - 1)).astype(
        jnp.bfloat16
    )
    pred_out = (out_weight[0] - LEARN_RATE * lag_value * direction(m_out, v_out, STEP - 1)).astype(
        jnp.bfloat16
    )
    full_in, full_out = (
        lax.all_gather(pred_in, "dp", axis=1, tiled=True),
        lax.all_gather(pred_out, "dp", axis=1, tiled=True),
    )
    normed, factor, values = normalize(forward_input[0], gain)
    gate_val = jnp.dot(normed, full_in[0], preferred_element_type=jnp.float32)
    up_val = jnp.dot(normed, full_in[1], preferred_element_type=jnp.float32)
    hidden = (gate_val * jax.nn.sigmoid(gate_val) * up_val).astype(jnp.bfloat16)
    partial_value = jnp.dot(hidden, full_out, preferred_element_type=jnp.float32)
    back_in, back_out = (full_in, full_out)
    out_cot = output_grad[0]
    normed_b, factor_b, values_b = normalize(backward_input[0], gain)
    gate_b = jnp.dot(normed_b, back_in[0], preferred_element_type=jnp.float32)
    up_b = jnp.dot(normed_b, back_in[1], preferred_element_type=jnp.float32)
    sig_b = jax.nn.sigmoid(gate_b)
    hidden_b = (gate_b * sig_b * up_b).astype(jnp.bfloat16)
    grad_h = jnp.dot(out_cot, back_out.T, preferred_element_type=jnp.float32)
    grad_gate = (grad_h * up_b * sig_b * (1.0 + gate_b * (1.0 - sig_b))).astype(jnp.bfloat16)
    grad_up = (grad_h * gate_b * sig_b).astype(jnp.bfloat16)
    grad_part = jnp.dot(grad_gate, back_in[0].T, preferred_element_type=jnp.float32) + jnp.dot(
        grad_up, back_in[1].T, preferred_element_type=jnp.float32
    )
    summed, grad_n = (
        lax.psum(partial_value.astype(jnp.bfloat16), "hid").astype(jnp.float32),
        lax.psum(grad_part.astype(jnp.bfloat16), "hid").astype(jnp.float32),
    )
    ahead = (values + summed).astype(jnp.bfloat16)
    next_rows = passed_along(ahead, "section", 1)
    scaled = gain * grad_n
    grad_x = (
        out_cot.astype(jnp.float32)
        + factor_b * scaled
        - values_b * factor_b**3 * jnp.mean(scaled * values_b, axis=-1, keepdims=True)
    )
    back_rows = passed_along(grad_x.astype(jnp.bfloat16), "section", -1)
    local_in = jnp.stack(
        [
            jnp.dot(normed_b.T, grad_gate, preferred_element_type=jnp.float32),
            jnp.dot(normed_b.T, grad_up, preferred_element_type=jnp.float32),
        ]
    )
    local_out = jnp.dot(hidden_b.T, out_cot, preferred_element_type=jnp.float32)
    sum_in, sum_out = (
        lax.psum_scatter(
            local_in.astype(jnp.bfloat16), "dp", scatter_dimension=1, tiled=True
        ).astype(jnp.float32),
        lax.psum_scatter(
            local_out.astype(jnp.bfloat16), "dp", scatter_dimension=1, tiled=True
        ).astype(jnp.float32),
    )
    rows_all = out_cot.shape[0] * lax.axis_size("dp")
    grad_in = sum_in / rows_all
    grad_out = sum_out / rows_all
    new_m_in = BETA_ONE * m_in + (1.0 - BETA_ONE) * grad_in
    new_v_in = BETA_TWO * v_in + (1.0 - BETA_TWO) * grad_in * grad_in
    new_m_out = BETA_ONE * m_out + (1.0 - BETA_ONE) * grad_out
    new_v_out = BETA_TWO * v_out + (1.0 - BETA_TWO) * grad_out * grad_out
    in_update = direction(new_m_in, new_v_in, STEP)
    out_update = direction(new_m_out, new_v_out, STEP)
    return (next_rows[None], back_rows[None], in_update[None], out_update[None])


def solution(mesh):
    in_specs = (
        P("section", "dp", None),
        P("section", "dp", None),
        P("section", "dp", None),
        P("section", None),
        P("section", None, "dp", "hid"),
        P("section", "hid", "dp"),
        P("section", None, "dp", "hid"),
        P("section", "hid", "dp"),
        P("section", None, None, "dp", "hid"),
        P("section", None, "hid", "dp"),
        P("section"),
    )
    out_specs = (
        P("section", "dp", None),
        P("section", "dp", None),
        P("section", None, "dp", "hid"),
        P("section", "hid", "dp"),
    )
    return jax.shard_map(local, mesh=mesh, in_specs=in_specs, out_specs=out_specs, check_vma=False)
```

profile of v0, /device:TPU:0, one launch (start us, length us, event | category | flops | bytes accessed | tf_op | source)
XLA Modules:
  0.0 193.6 jit_solution(17537712004479626247)
XLA Ops:
  7.2 0.0 all-gather.3.cloned.1.call-start
  7.9 0.7 fusion.87
  8.6 0.0 copy-start.13
  8.6 4.1 %fusion.40 = bf16[2,512,256]{2,1,0:T(8,128)(2,1)} fusion(f32[1,2,512,256]{3,2,1,0:T(8,128)} %param.15, f32[]{:T(128)} %bitcast.4, s32[1,2,512,256]{3,2,1,0:T(8,128)} %param.17, f32[2,512]{1,0:T(2,128)S(1)} %get-tuple-element.17, f32[2,512]{1,0:T(2,128)S(1)} %get-tuple-element.16), kind=kLoop, calls=%fused_computation.66 | loop fusion | flops 8912896 | bytes 2629636 | tf_op jit(solution)/shard_map/convert_element_type | solution.py:70
  12.7 0.0 all-gather.3.cloned.1.call-update
  12.7 0.0 reduce-scatter.5.cloned.1.call-start
  12.8 0.2 fusion.13
  13.0 37.7 %all-gather.3.cloned.1.call-done = bf16[2,2048,256]{2,1,0:T(8,128)(2,1)} async-done(((bf16[2,512,256]{2,1,0:T(8,128)(2,1)}), bf16[2,2048,256]{2,1,0:T(8,128)(2,1)}) %all-gather.3.cloned.1.call-update) | async-done | bytes 2097168 | tf_op jit(solution)/shard_map/all_gather | solution.py:77
  50.8 0.0 copy-done.13
  50.8 1.8 fusion.45
  52.6 0.1 copy-done.5
  52.7 0.4 fusion.43
  53.1 0.8 copy-done.3
  53.9 1.5 convolution_convert_fusion
  55.4 0.0 copy-done.9
  55.4 0.0 reduce-scatter.5.cloned.1.call-update
  55.4 0.0 all-gather.5.cloned.1.call-start
  55.5 28.0 %reduce-scatter.5.cloned.1.call-done = bf16[256,512]{1,0:T(8,128)(2,1)} async-done(((bf16[256,2048]{1,0:T(8,128)(2,1)}), bf16[256,512]{1,0:T(8,128)(2,1)}) %reduce-scatter.5.cloned.1.call-update) | async-done | bytes 262160 | tf_op jit(solution)/shard_map/reduce_scatter | solution.py:122
  83.5 3.0 %fusion.61 = (f32[1,256,512]{2,1,0:T(8,128)}, bf16[256,512]{1,0:T(8,128)(2,1)}) fusion(bf16[256,512]{1,0:T(8,128)(2,1)} %reduce-scatter.5.cloned.1.call-done, s32[1,256,512]{2,1,0:T(8,128)S(1)} %copy-done.7, f32[512]{0:T(512)S(1)} %bitcast.177, f32[512]{0:T(512)S(1)} %bitcast.176, f32[]{:T(128)} %bitcast.4, f32[1,256,512]{2,1,0:T(8,128)S(1)} %copy-done.8), kind=kLoop, calls=%fused_computation.95 | loop fusion | flops 6029312 | bytes 2101252 | tf_op jit(solution)/shard_map/broadcast_in_dim | solution.py:135
  86.5 0.0 all-gather.5.cloned.1.call-update
  86.5 0.0 all-reduce.3.cloned.1.call-start
  86.6 0.2 fusion.9
  86.8 0.0 copy-start.12
  86.8 1.7 fusion.44
  88.6 24.5 %all-gather.5.cloned.1.call-done = bf16[256,2048]{1,0:T(8,128)(2,1)} async-done(((bf16[256,512]{1,0:T(8,128)(2,1)}), bf16[256,2048]{1,0:T(8,128)(2,1)}) %all-gather.5.cloned.1.call-update) | async-done | bytes 1048592 | tf_op jit(solution)/shard_map/all_gather | solution.py:78
  113.0 1.7 multiply_convert_fusion.1
  114.8 3.5 %convolution_convert_fusion.3 = bf16[192,2048]{1,0:T(8,128)(2,1)} fusion(bf16[256,2048]{1,0:T(8,128)(2,1)} %all-gather.5.cloned.1.call-done, bf16[2,2048,256]{2,1,0:T(8,128)(2,1)} %all-gather.3.cloned.1.call-done, bf16[1,192,2048]{2,1,0:T(8,128)(2,1)S(1)} %copy-done.2, f32[2048]{0:T(1024)S(1)} %bitcast.171, f32[192]{0:T(256)S(1)} %add_rsqrt_fusion.1, ...), kind=kOutput, calls=%fused_computation.5 | convolution fusion | flops 404914176 | bytes 3875584 | tf_op jit(solution)/shard_map/dot_general | solution.py:84
  118.3 1.9 fusion.42
  120.2 0.0 copy-done.6
  120.2 1.4 fusion
  121.6 0.0 all-reduce.3.cloned.1.call-update
  121.6 0.0 reduce-scatter.3.cloned.1.call-start
  121.7 0.6 fusion.2
  122.3 0.6 fusion.1
  122.8 1.5 pad_maximum_fusion
  124.3 0.0 reduce-scatter.3.cloned.1.call-update
  124.4 17.8 %all-reduce.3.cloned.1.call-done = (bf16[192,2048]{1,0:T(8,128)(2,1)}, bf16[192,2048]{1,0:T(8,128)(2,1)}) async-done(((bf16[192,2048]{1,0:T(8,128)(2,1)}, bf16[192,2048]{1,0:T(8,128)(2,1)}), (bf16[192,2048]{1,0:T(8,128)(2,1)}, bf16[192,2048]{1,0:T(8,128)(2,1)})) %all-reduce.3.cloned.1.call-update) | async-done | bytes 1572880 | tf_op jit(solution)/shard_map/psum | solution.py:99
  142.2 1.5 fusion.10
  143.7 3.7 %collective-permute-start = (bf16[192,2048]{1,0:T(8,128)(2,1)S(1)}, bf16[192,2048]{1,0:T(8,128)(2,1)S(1)}, u32[]{:S(2)}, u32[]{:S(2)}) collective-permute-start(bf16[192,2048]{1,0:T(8,128)(2,1)S(1)} %fusion.10), channel_id=1, source_target_pairs={{0,8},{8,16},{16,24},{1,9},{9,17},{17,25},{2,10},{10,18},{18,26},{... | collective-permute-start | bytes 2359304 | tf_op jit(solution)/shard_map/ppermute | solution.py:20
  147.4 0.3 fusion.17
  147.8 0.6 fusion.16
  148.4 1.3 collective-permute-start.1
  149.7 14.9 %collective-permute-done = bf16[192,2048]{1,0:T(8,128)(2,1)S(1)} collective-permute-done((bf16[192,2048]{1,0:T(8,128)(2,1)S(1)}, bf16[192,2048]{1,0:T(8,128)(2,1)S(1)}, u32[]{:S(2)}, u32[]{:S(2)}) %collective-permute-start) | collective-permute-done | bytes 786464 | tf_op jit(solution)/shard_map/ppermute | solution.py:20
  164.6 5.1 %collective-permute-done.1 = bf16[192,2048]{1,0:T(8,128)(2,1)S(1)} collective-permute-done((bf16[192,2048]{1,0:T(8,128)(2,1)S(1)}, bf16[192,2048]{1,0:T(8,128)(2,1)S(1)}, u32[]{:S(2)}, u32[]{:S(2)}) %collective-permute-start.1) | collective-permute-done | bytes 786464 | tf_op jit(solution)/shard_map/ppermute | solution.py:20
  169.7 11.7 %reduce-scatter.3.cloned.1.call-done = bf16[2,512,256]{2,1,0:T(8,128)(2,1)} async-done(((bf16[2,2048,256]{2,1,0:T(8,128)(2,1)}), bf16[2,512,256]{2,1,0:T(8,128)(2,1)}) %reduce-scatter.3.cloned.1.call-update) | async-done | bytes 524304 | tf_op jit(solution)/shard_map/reduce_scatter | solution.py:119
  181.4 3.9 %fusion.33 = f32[1,2,512,256]{3,2,1,0:T(8,128)} fusion(bf16[2,512,256]{2,1,0:T(8,128)(2,1)} %reduce-scatter.3.cloned.1.call-done, s32[1,2,512,256]{3,2,1,0:T(8,128)S(1)} %copy-done.1, f32[2,512]{1,0:T(2,128)S(1)} %get-tuple-element.17, f32[2,512]{1,0:T(2,128)S(1)} %get-tuple-element.16), kind=kLoop, calls=%fused_computation.54 | loop fusion | flops 10223616 | bytes 2629632 | tf_op jit(solution)/shard_map/broadcast_in_dim | solution.py:135
  185.3 0.9 copy.24
  186.2 0.9 copy.25
  (28 shorter events, 0.1 us)
Async XLA Ops:
  7.2 43.6 %all-gather.3.cloned.1.call-start = ((), (), s32[]{:S(2)}) async-start(), calls=%async_computation.2 | async-start | bytes 2621440 | tf_op jit(solution)/shard_map/all_gather | solution.py:77
  8.6 4.2 %copy-start = (bf16[1,192,2048]{2,1,0:T(8,128)(2,1)S(1)}, bf16[1,192,2048]{2,1,0:T(8,128)(2,1)}, u32[]{:S(2)}) copy-start(bf16[1,192,2048]{2,1,0:T(8,128)(2,1)} %param.12) | copy-start | bytes 2359300
  8.6 42.2 %copy-start.13 = (f32[1,2048]{1,0:T(1,128)S(1)}, f32[1,2048]{1,0:T(1,128)}, u32[]{:S(2)}) copy-start(f32[1,2048]{1,0:T(1,128)} %param.14) | copy-start | bytes 24580
  12.7 70.8 %reduce-scatter.5.cloned.1.call-start = ((), (), s32[]{:S(2)}) async-start(), calls=%async_computation.5 | async-start | bytes 1310720 | tf_op jit(solution)/shard_map/reduce_scatter | solution.py:122
  50.8 1.9 copy-start.5
  52.7 2.7 %copy-start.9 = (f32[192,256]{1,0:T(8,128)}, f32[192,256]{1,0:T(8,128)S(1)}, u32[]{:S(2)}) copy-start(f32[192,256]{1,0:T(8,128)S(1)} %fusion.45) | copy-start | bytes 589828
  52.7 1.2 copy-start.3
  53.9 1.5 copy-start.11
  53.9 1.6 copy-start.14
  53.9 29.6 %copy-start.7 = (s32[1,256,512]{2,1,0:T(8,128)S(1)}, s32[1,256,512]{2,1,0:T(8,128)}, u32[]{:S(2)}) copy-start(s32[1,256,512]{2,1,0:T(8,128)} %param.18) | copy-start | bytes 1572868
  53.9 29.6 %copy-start.8 = (f32[1,256,512]{2,1,0:T(8,128)S(1)}, f32[1,256,512]{2,1,0:T(8,128)}, u32[]{:S(2)}) copy-start(f32[1,256,512]{2,1,0:T(8,128)} %param.16) | copy-start | bytes 1572868
  55.4 31.2 %copy-start.2 = (bf16[1,192,2048]{2,1,0:T(8,128)(2,1)S(1)}, bf16[1,192,2048]{2,1,0:T(8,128)(2,1)}, u32[]{:S(2)}) copy-start(bf16[1,192,2048]{2,1,0:T(8,128)(2,1)} %param.11) | copy-start | bytes 2359300
  55.4 57.6 %all-gather.5.cloned.1.call-start = ((), (), s32[]{:S(2)}) async-start(), calls=%async_computation.3 | async-start | bytes 1310720 | tf_op jit(solution)/shard_map/all_gather | solution.py:78
  86.5 55.7 %all-reduce.3.cloned.1.call-start = ((), (), s32[]{:S(2)}) async-start(), calls=%async_computation.6 | async-start | bytes 3145728 | tf_op jit(solution)/shard_map/psum | solution.py:99
  86.8 26.2 %copy-start.10 = (f32[192,256]{1,0:T(8,128)S(1)}, f32[192,256]{1,0:T(8,128)}, u32[]{:S(2)}) copy-start(f32[192,256]{1,0:T(8,128)} %copy-done.9) | copy-start | bytes 589828
  86.8 26.2 %copy-start.12 = (f32[192,256]{1,0:T(8,128)S(1)}, f32[192,256]{1,0:T(8,128)}, u32[]{:S(2)}) copy-start(f32[192,256]{1,0:T(8,128)} %copy-done.11) | copy-start | bytes 589828
  118.3 1.9 copy-start.6
  121.6 59.8 %reduce-scatter.3.cloned.1.call-start = ((), (), s32[]{:S(2)}) async-start(), calls=%async_computation.4 | async-start | bytes 2621440 | tf_op jit(solution)/shard_map/reduce_scatter | solution.py:119
  142.2 5.2 %copy-start.4 = (bf16[192,2048]{1,0:T(8,128)(2,1)S(1)}, bf16[192,2048]{1,0:T(8,128)(2,1)}, u32[]{:S(2)}) copy-start(bf16[192,2048]{1,0:T(8,128)(2,1)} %get-tuple-element.5) | copy-start | bytes 2359300
  143.7 20.9 %collective-permute-start = (bf16[192,2048]{1,0:T(8,128)(2,1)S(1)}, bf16[192,2048]{1,0:T(8,128)(2,1)S(1)}, u32[]{:S(2)}, u32[]{:S(2)}) collective-permute-start(bf16[192,2048]{1,0:T(8,128)(2,1)S(1)} %fusion.10), channel_id=1, source_target_pairs={{0,8},{8,16},{16,24},{1,9},{9,17},{17,25},{2,10},{10,18},{18,26},{... | collective-permute-start | bytes 2359304 | tf_op jit(solution)/shard_map/ppermute | solution.py:20
  147.8 33.6 %copy-start.1 = (s32[1,2,512,256]{3,2,1,0:T(8,128)S(1)}, s32[1,2,512,256]{3,2,1,0:T(8,128)}, u32[]{:S(2)}) copy-start(s32[1,2,512,256]{3,2,1,0:T(8,128)} %param.17) | copy-start | bytes 3145732
  148.4 21.3 %collective-permute-start.1 = (bf16[192,2048]{1,0:T(8,128)(2,1)S(1)}, bf16[192,2048]{1,0:T(8,128)(2,1)S(1)}, u32[]{:S(2)}, u32[]{:S(2)}) collective-permute-start(bf16[192,2048]{1,0:T(8,128)(2,1)S(1)} %fusion.16), channel_id=1, source_target_pairs={{8,0},{16,8},{24,16},{9,1},{17,9},{25,17},{10,2},{18,10},{26,18},{... | collective-permute-start | bytes 2359304 | tf_op jit(solution)/shard_map/ppermute | solution.py:20
Sparse Core Ops, SparseCore 0:
  12.8 37.8 all-gather.2
  55.5 27.9 reduce-scatter.4
  86.6 26.3 all-gather.4
  121.7 20.4 all-reduce.2
  145.0 36.3 reduce-scatter.2
where the time goes:
time: 194 us
  waiting for transfers between devices  140 us (72%)
  other arithmetic  15.4 us (8%)
  matrix products  15.1 us (8%)
  between operations  14.6 us (8%)
  starting transfers between devices  5.21 us (3%)
  local copies, waits for them, and re-layouts  3.42 us (2%)
    all_gather x1, waiting for transfers between devices, local(): lax.all_gather(pred_in, 'dp', axis=1, tiled=True)  37.7 us
    reduce_scatter x1, waiting for transfers between devices, local(): lax.psum_scatter(local_out.astype(jnp.bfloat16), 'dp', scatter_dimension=...  28 us
    all_gather x1, waiting for transfers between devices, local(): lax.all_gather(pred_out, 'dp', axis=1, tiled=True)  24.5 us
    ppermute x2, waiting for transfers between devices, passed_along(): return lax.ppermute(block, axis, route)  20 us
    psum x1, waiting for transfers between devices, local(): lax.psum(partial_value.astype(jnp.bfloat16), 'hid').astype(jnp.float32)  17.8 us
    reduce_scatter x1, waiting for transfers between devices, local(): lax.psum_scatter(local_in.astype(jnp.bfloat16), 'dp', scatter_dimension=1...  11.7 us
    broadcast_in_dim x2, other arithmetic, local(): return (next_rows[None], back_rows[None], in_update[None], out_update[None])  6.92 us
    ppermute x2, starting transfers between devices, passed_along(): return lax.ppermute(block, axis, route)  5.01 us
  transfers between devices with their start and end apart: 7, of which 7 were waited for; matrix products, arithmetic and copies ran while one was open for 4% of the time, Pallas kernels for 0%

commit v1 on v0

--- a/solution.py
+++ b/solution.py
@@ -1,6 +1,11 @@
+import functools
+import math
+
 import jax
 import jax.numpy as jnp
 from jax import lax
+from jax.experimental import pallas as pl
+from jax.experimental.pallas import tpu as pltpu
 from jax.sharding import PartitionSpec as P
 
 QB = 256
@@ -12,6 +17,8 @@
 ADAM_EPS = 1e-08
 NORM_EPS = 1e-06
 LEARN_RATE = 0.003
+MESH = pl.DeviceIdType.MESH
+CHUNKS = 2
 
 
 def passed_along(block, axis, distance):
@@ -135,6 +142,500 @@
     return (next_rows[None], back_rows[None], in_update[None], out_update[None])
 
 
+def matmul(a, b):
+    return jnp.dot(a, b, preferred_element_type=jnp.float32)
+
+
+def matmul_nt(a, b):
+    return lax.dot_general(a, b, (((1,), (1,)), ((), ())), preferred_element_type=jnp.float32)
+
+
+def matmul_tn(a, b):
+    return lax.dot_general(a, b, (((0,), (0,)), ((), ())), preferred_element_type=jnp.float32)
+
+
+def moments(codes, first_scale, second_scale):
+    high = (codes >> 8).astype(jnp.float32)
+    low = (codes & 255).astype(jnp.float32)
+    moment_m = first_scale * ((high - 63.0) * (1.0 / 63.0))
+    root_v = second_scale * (0.25 + low * (0.75 / 255.0))
+    return moment_m, root_v
+
+
+def predicted(weight, codes, first_scale, second_scale, step):
+    moment_m, root_v = moments(codes, first_scale, second_scale)
+    count = STEP - 1
+    top = moment_m * (step / (1.0 - BETA_ONE**count))
+    bottom = root_v * (1.0 / math.sqrt(1.0 - BETA_TWO**count)) + ADAM_EPS
+    return (weight - top / bottom).astype(jnp.bfloat16)
+
+
+def updated(grad, codes, first_scale, second_scale):
+    moment_m, root_v = moments(codes, first_scale, second_scale)
+    new_m = BETA_ONE * moment_m + (1.0 - BETA_ONE) * grad
+    new_v = BETA_TWO * (root_v * root_v) + (1.0 - BETA_TWO) * grad * grad
+    bottom = jnp.sqrt(new_v * (1.0 / (1.0 - BETA_TWO**STEP))) + ADAM_EPS
+    return new_m * (1.0 / (1.0 - BETA_ONE**STEP)) / bottom
+
+
+def tick_kernel(
+    n_sec,
+    lag_ref, gain_ref, s_in_ref, s_out_ref,
+    xf_hbm, xb_hbm, dy_hbm, w_in_hbm, w_out_hbm, c_in_hbm, c_out_hbm,
+    y_out, dx_out, u_in_out, u_out_out,
+    xf, xb, dy, w_in, w_out, c_in, c_out, s_t,
+    p_in, p_out, nrm, acc, dh, hid, dgdu, h_all, n_all, dy_all,
+    q_s, q_r, e_s, e_r, y_s, dx_s, y_b, dx_b, g_in, g_out,
+    load_sem, store_sem, send_sem, recv_sem,
+):
+    sec = lax.axis_index("section")
+    me = lax.axis_index("dp")
+    core = lax.axis_index("hid")
+    n_dp, rows, cols = xf.shape
+    ff = w_out.shape[0]
+    half_r = rows // 2
+    me_x = me + 1 - 2 * (me % 2)
+    me_y = (me + 2) % 4
+    me_d = 3 - me
+    owners = (me, me_x, me_y, me_d)
+    dev_x, dev_y, dev_d = ((sec, o, core) for o in owners[1:])
+    sibling = (sec, me, 1 - core)
+    above = (sec + 1, me, core)
+    below = (sec - 1, me, core)
+
+    ids = iter(range(send_sem.shape[0]))
+
+    def remote(src, dst, dev):
+        i = next(ids)
+        return pltpu.make_async_remote_copy(
+            src_ref=src, dst_ref=dst, send_sem=send_sem.at[i], recv_sem=recv_sem.at[i],
+            device_id=dev, device_id_type=MESH,
+        )
+
+    lids = iter(range(load_sem.shape[0]))
+
+    def load(src, dst):
+        copy = pltpu.make_async_copy(src, dst, load_sem.at[next(lids)])
+        copy.start()
+        return copy
+
+    def load_cols(src, dst):
+        return [load(src.at[:, pl.ds(j * cols, cols)], dst.at[j]) for j in range(n_dp)]
+
+    l_in = [load(c_in_hbm, c_in), load(w_in_hbm, w_in)]
+    l_out = [load(c_out_hbm, c_out), load(w_out_hbm, w_out)]
+    l_xb = load_cols(xb_hbm, xb)
+    l_xf = load_cols(xf_hbm, xf)
+    l_dy = load_cols(dy_hbm, dy)
+
+    barrier = pltpu.get_barrier_semaphore()
+    for dev in (dev_x, dev_y, dev_d, sibling):
+        pl.semaphore_signal(barrier, inc=1, device_id=dev, device_id_type=MESH)
+
+    @pl.when(sec < n_sec - 1)
+    def _():
+        pl.semaphore_signal(barrier, inc=1, device_id=above, device_id_type=MESH)
+
+    @pl.when(sec > 0)
+    def _():
+        pl.semaphore_signal(barrier, inc=1, device_id=below, device_id_type=MESH)
+
+    step = LEARN_RATE * lag_ref[0].astype(jnp.float32)
+    for i in range(4):
+        s_t[i] = jnp.transpose(jnp.broadcast_to(s_in_ref[i : i + 1, :], (128, cols)))
+    reps = ff // 128
+
+    def row_scale(i, at):
+        return jnp.concatenate([s_t[i, at, :]] * reps, axis=1)
+
+    for c in l_in:
+        c.wait()
+
+    def predict_in(start):
+        @pl.loop(0, cols // 2 // 32)
+        def _(t):
+            at = pl.ds(pl.multiple_of(start + t * 32, 32), 32)
+            for k in range(2):
+                p_in[0, at, k * ff : (k + 1) * ff] = predicted(
+                    w_in[k, at, :], c_in[k, at, :], row_scale(k, at), row_scale(2 + k, at), step
+                )
+
+    hc = cols // 2
+    hf = ff // 2
+    lo, hi = pl.ds(0, hc), pl.ds(hc, hc)
+    flo, fhi = pl.ds(0, hf), pl.ds(hf, hf)
+    rlo, rhi = pl.ds(0, half_r), pl.ds(half_r, half_r)
+
+    def spread(buf, first, second):
+        to_x = [remote(buf.at[0, p], buf.at[1, p], dev_x) for p in (first, second)]
+        to_y = [remote(buf.at[0, p], buf.at[2, p], dev_y) for p in (first, second)]
+        on_y = remote(buf.at[1, first], buf.at[3, first], dev_y)
+        on_x = remote(buf.at[2, second], buf.at[3, second], dev_x)
+        return to_x, to_y, on_y, on_x
+
+    a_x, a_y, a_on_y, a_on_x = spread(p_in, lo, hi)
+    d_x, d_y, d_on_y, d_on_x = spread(p_out, flo, fhi)
+    h_x, h_y, h_on_y, h_on_x = spread(h_all, rlo, rhi)
+    g_x, g_y, g_on_y, g_on_x = spread(dgdu, rlo, rhi)
+
+    predict_in(0)
+    expect = 4 + jnp.where(sec > 0, 1, 0) + jnp.where(sec < n_sec - 1, 1, 0)
+    pl.semaphore_wait(barrier, expect)
+    a_x[0].start()
+    a_y[0].start()
+    predict_in(hc)
+    a_y[1].start()
+    a_x[1].start()
+
+    for c in l_out:
+        c.wait()
+    sm, sv = s_out_ref[0:1, :], s_out_ref[1:2, :]
+
+    @pl.loop(0, ff // 32)
+    def _(t):
+        at = pl.ds(pl.multiple_of(t * 32, 32), 32)
+        p_out[0, at, :] = predicted(w_out[at, :], c_out[at, :], sm, sv, step)
+
+    d_x[0].start()
+    d_y[1].start()
+    d_x[1].start()
+    d_y[0].start()
+
+    gain = gain_ref[...]
+
+    def normalize(src, base):
+        @pl.loop(0, rows // 16)
+        def _(t):
+            at = pl.ds(pl.multiple_of(t * 16, 16), 16)
+            to = pl.ds(pl.multiple_of(base + t * 16, 16), 16)
+            parts = [src[j, at, :].astype(jnp.float32) for j in range(n_dp)]
+            total = functools.reduce(jnp.add, [p * p for p in parts])
+            factor = lax.rsqrt(
+                jnp.sum(total, axis=-1, keepdims=True) * (1.0 / (n_dp * cols)) + NORM_EPS
+            )
+            for j in range(n_dp):
+                scaled = parts[j] * factor * gain[:, j * cols : (j + 1) * cols]
+                nrm[j, to, :] = scaled.astype(jnp.bfloat16)
+
+    for c in l_xb:
+        c.wait()
+    normalize(xb, rows)
+    for c in l_xf:
+        c.wait()
+    normalize(xf, 0)
+    for c in l_dy:
+        c.wait()
+    acc[...] = matmul(nrm[me], p_in[0])
+    dh[...] = matmul_nt(dy[me], p_out[0])
+    n_all[0] = nrm[me, rows:, :]
+    dy_all[0] = dy[me]
+
+    a_x[0].wait_recv()
+    a_on_y.start()
+    a_y[1].wait_recv()
+    a_on_x.start()
+    a_x[1].wait_recv()
+    acc[...] += matmul(nrm[me_x], p_in[1])
+    a_y[0].wait_recv()
+    acc[...] += matmul(nrm[me_y], p_in[2])
+    d_x[0].wait_recv()
+    d_on_y.start()
+    d_y[1].wait_recv()
+    d_on_x.start()
+
+    mine = pl.ds(pl.multiple_of(core * half_r, half_r), half_r)
+    mine_b = pl.ds(pl.multiple_of(rows + core * half_r, half_r), half_r)
+    share = []
+    for slot, owner, dev in ((1, me_x, dev_x), (2, me_y, dev_y), (3, me_d, dev_d)):
+        share.append((
+            remote(dy.at[owner, mine], dy_all.at[slot, mine], dev),
+            remote(dy_all.at[slot, mine], dy_all.at[slot, mine], sibling),
+        ))
+        share.append((
+            remote(nrm.at[owner, mine_b], n_all.at[slot, mine], dev),
+            remote(n_all.at[slot, mine], n_all.at[slot, mine], sibling),
+        ))
+    for c, _ in share:
+        c.start()
+
+    d_x[1].wait_recv()
+    dh[...] += matmul_nt(dy[me_x], p_out[1])
+    d_y[0].wait_recv()
+    dh[...] += matmul_nt(dy[me_y], p_out[2])
+
+    a_on_y.wait_recv()
+    a_on_x.wait_recv()
+    acc[...] += matmul(nrm[me_d], p_in[3])
+
+    @pl.loop(0, rows // 32)
+    def _(t):
+        at = pl.ds(pl.multiple_of(t * 32, 32), 32)
+        gate, up = acc[at, :ff], acc[at, ff:]
+        hid[at, :] = (gate * jax.nn.sigmoid(gate) * up).astype(jnp.bfloat16)
+        to = pl.ds(pl.multiple_of(rows + t * 32, 32), 32)
+        gate, up = acc[to, :ff], acc[to, ff:]
+        h_all[0, at, :] = (gate * jax.nn.sigmoid(gate) * up).astype(jnp.bfloat16)
+
+    for c in (h_x[0], h_y[1], h_x[1], h_y[0]):
+        c.start()
+    hidden = hid[...]
+    for slot in range(3):
+        q_s[owners[slot]] = matmul(hidden, p_out[slot]).astype(jnp.bfloat16)
+    d_on_y.wait_recv()
+    d_on_x.wait_recv()
+    dh[...] += matmul_nt(dy[me_d], p_out[3])
+
+    @pl.loop(0, rows // 32)
+    def _(t):
+        at = pl.ds(pl.multiple_of(t * 32, 32), 32)
+        to = pl.ds(pl.multiple_of(rows + t * 32, 32), 32)
+        gate, up, grad = acc[to, :ff], acc[to, ff:], dh[at, :]
+        sig = jax.nn.sigmoid(gate)
+        dgdu[0, at, :ff] = (grad * up * sig * (1.0 + gate * (1.0 - sig))).astype(jnp.bfloat16)
+        dgdu[0, at, ff:] = (grad * gate * sig).astype(jnp.bfloat16)
+
+    for c in (g_x[0], g_y[1], g_x[1], g_y[0]):
+        c.start()
+
+    part = half_r // CHUNKS
+    other = pl.multiple_of((1 - core) * half_r, half_r)
+    own = pl.multiple_of(core * half_r, half_r)
+
+    def swaps(src, dst):
+        return [
+            remote(
+                src.at[:, pl.ds(pl.multiple_of(other + c * part, part), part)],
+                dst.at[:, pl.ds(c * part, part)], sibling,
+            )
+            for c in range(CHUNKS)
+        ]
+
+    q_x, e_x = swaps(q_s, q_r), swaps(e_s, e_r)
+
+    def moved(src, dst, dev):
+        pairs = []
+        for c in range(CHUNKS):
+            at = pl.ds(pl.multiple_of(own + c * part, part), part)
+            pairs.append((
+                remote(src.at[pl.ds(c * part, part)], dst.at[at], dev),
+                remote(dst.at[at], dst.at[at], sibling),
+            ))
+        return pairs
+
+    y_m, dx_m = moved(y_s, y_b, above), moved(dx_s, dx_b, below)
+    first, last = sec == 0, sec == n_sec - 1
+
+    q_s[me_d] = matmul(hidden, p_out[3]).astype(jnp.bfloat16)
+    for c in q_x:
+        c.start()
+    back = dgdu[0]
+    for slot in range(4):
+        e_s[owners[slot]] = matmul_nt(back, p_in[slot]).astype(jnp.bfloat16)
+    for c in e_x:
+        c.start()
+
+    for c in range(CHUNKS):
+        q_x[c].wait_recv()
+
+        @pl.loop(0, part // 16)
+        def _(t, c=c):
+            at = pl.ds(pl.multiple_of(own + c * part + t * 16, 16), 16)
+            near = pl.ds(pl.multiple_of(c * part + t * 16, 16), 16)
+            for j in range(n_dp):
+                total = q_s[j, at, :].astype(jnp.float32) + q_r[j, near, :].astype(jnp.float32)
+                y_s[near, j * cols : (j + 1) * cols] = (
+                    xf[j, at, :].astype(jnp.float32) + total
+                ).astype(jnp.bfloat16)
+
+        @pl.when(jnp.logical_not(last))
+        def _(c=c):
+            y_m[c][0].start()
+
+    for c in range(CHUNKS):
+        e_x[c].wait_recv()
+
+        @pl.loop(0, part // 16)
+        def _(t, c=c):
+            at = pl.ds(pl.multiple_of(own + c * part + t * 16, 16), 16)
+            near = pl.ds(pl.multiple_of(c * part + t * 16, 16), 16)
+            xs = [xb[j, at, :].astype(jnp.float32) for j in range(n_dp)]
+            total = functools.reduce(jnp.add, [p * p for p in xs])
+            inv = 1.0 / (n_dp * cols)
+            factor = lax.rsqrt(jnp.sum(total, axis=-1, keepdims=True) * inv + NORM_EPS)
+            scaled = [
+                gain[:, j * cols : (j + 1) * cols]
+                * (e_s[j, at, :].astype(jnp.float32) + e_r[j, near, :].astype(jnp.float32))
+                for j in range(n_dp)
+            ]
+            inner = functools.reduce(jnp.add, [s * x for s, x in zip(scaled, xs)])
+            mean = jnp.sum(inner, axis=-1, keepdims=True) * inv
+            tail = factor * factor * factor * mean
+            for j in range(n_dp):
+                dx_s[near, j * cols : (j + 1) * cols] = (
+                    dy[j, at, :].astype(jnp.float32) + factor * scaled[j] - xs[j] * tail
+                ).astype(jnp.bfloat16)
+
+        @pl.when(jnp.logical_not(first))
+        def _(c=c):
+            dx_m[c][0].start()
+
+    for c, on in share:
+        c.wait_recv()
+        on.start()
+    h_x[0].wait_recv()
+    h_on_y.start()
+    h_y[1].wait_recv()
+    h_on_x.start()
+    g_x[0].wait_recv()
+    g_on_y.start()
+    g_y[1].wait_recv()
+    g_on_x.start()
+
+    @pl.when(first)
+    def _():
+        y_b[...] = jnp.zeros_like(y_b)
+
+    @pl.when(jnp.logical_not(first))
+    def _():
+        for c, on in y_m:
+            c.wait_recv()
+            on.start()
+
+    @pl.when(last)
+    def _():
+        dx_b[...] = jnp.zeros_like(dx_b)
+
+    @pl.when(jnp.logical_not(last))
+    def _():
+        for c, on in dx_m:
+            c.wait_recv()
+            on.start()
+
+    for _, on in share:
+        on.wait_recv()
+    h_x[1].wait_recv()
+    h_y[0].wait_recv()
+    h_on_y.wait_recv()
+    h_on_x.wait_recv()
+    tokens = n_dp * rows
+    share_of = 1.0 / tokens
+    g_out[...] = matmul_tn(h_all[...].reshape(tokens, ff), dy_all[...].reshape(tokens, cols))
+
+    @pl.loop(0, ff // 32)
+    def _(t):
+        at = pl.ds(pl.multiple_of(t * 32, 32), 32)
+        g_out[at, :] = updated(g_out[at, :] * share_of, c_out[at, :], sm, sv)
+
+    store_ids = iter(range(store_sem.shape[0]))
+
+    def store(src, dst):
+        copy = pltpu.make_async_copy(src, dst, store_sem.at[next(store_ids)])
+        copy.start()
+        return copy
+
+    stores = [store(g_out, u_out_out)]
+
+    g_x[1].wait_recv()
+    g_y[0].wait_recv()
+    g_on_y.wait_recv()
+    g_on_x.wait_recv()
+    grad_in = matmul_tn(n_all[...].reshape(tokens, cols), dgdu[...].reshape(tokens, 2 * ff))
+    for k in range(2):
+        g_in[k] = grad_in[:, k * ff : (k + 1) * ff]
+
+    @pl.loop(0, cols // 32)
+    def _(t):
+        at = pl.ds(pl.multiple_of(t * 32, 32), 32)
+        for k in range(2):
+            g_in[k, at, :] = updated(
+                g_in[k, at, :] * share_of, c_in[k, at, :], row_scale(k, at), row_scale(2 + k, at)
+            )
+
+    stores.append(store(g_in, u_in_out))
+
+    @pl.when(jnp.logical_not(first))
+    def _():
+        for c, on in y_m:
+            on.wait_recv()
+            on.wait_send()
+        for c, _ in dx_m:
+            c.wait_send()
+
+    @pl.when(jnp.logical_not(last))
+    def _():
+        for c, on in dx_m:
+            on.wait_recv()
+            on.wait_send()
+        for c, _ in y_m:
+            c.wait_send()
+
+    stores.append(store(y_b, y_out))
+    stores.append(store(dx_b, dx_out))
+    for group in ((a_x, a_y, a_on_y, a_on_x), (d_x, d_y, d_on_y, d_on_x),
+                  (h_x, h_y, h_on_y, h_on_x), (g_x, g_y, g_on_y, g_on_x)):
+        for c in (*group[0], *group[1], group[2], group[3]):
+            c.wait_send()
+    for c, on in share:
+        c.wait_send()
+        on.wait_send()
+    for c in (*q_x, *e_x):
+        c.wait_send()
+    for c in stores:
+        c.wait()
+
+
+def tick(
+    n_sec, n_dp,
+    forward_input, backward_input, output_grad, norm_gain,
+    in_weight, out_weight, in_codes, out_codes, in_scales, out_scales, section_lags,
+):
+    xf, xb, dy = forward_input[0], backward_input[0], output_grad[0]
+    rows, width = xf.shape
+    _, cols, ff = in_weight.shape[1:]
+    half_r = rows // 2
+    bf, f32 = jnp.bfloat16, jnp.float32
+    vmem = pl.BlockSpec(memory_space=pltpu.VMEM)
+    hbm = pl.BlockSpec(memory_space=pl.ANY)
+    V = pltpu.VMEM
+    wide = (n_dp, rows, cols)
+    n_remote = 4 * 6 + 12 + 2 * CHUNKS + 4 * CHUNKS
+    outs = pl.pallas_call(
+        functools.partial(tick_kernel, n_sec),
+        out_shape=(
+            jax.ShapeDtypeStruct((rows, width), bf),
+            jax.ShapeDtypeStruct((rows, width), bf),
+            jax.ShapeDtypeStruct((2, cols, ff), f32),
+            jax.ShapeDtypeStruct((ff, cols), f32),
+        ),
+        in_specs=[pl.BlockSpec(memory_space=pltpu.SMEM), vmem, vmem, vmem] + [hbm] * 7,
+        out_specs=(hbm,) * 4,
+        scratch_shapes=[
+            V(wide, bf), V(wide, bf), V(wide, bf),
+            V((2, cols, ff), f32), V((ff, cols), f32),
+            V((2, cols, ff), jnp.int32), V((ff, cols), jnp.int32),
+            V((4, cols, 128), f32),
+            V((n_dp, cols, 2 * ff), bf), V((n_dp, ff, cols), bf),
+            V((n_dp, 2 * rows, cols), bf),
+            V((2 * rows, 2 * ff), f32), V((rows, ff), f32), V((rows, ff), bf),
+            V((n_dp, rows, 2 * ff), bf), V((n_dp, rows, ff), bf), V(wide, bf), V(wide, bf),
+            V(wide, bf), V((n_dp, half_r, cols), bf), V(wide, bf), V((n_dp, half_r, cols), bf),
+            V((half_r, width), bf), V((half_r, width), bf), V((rows, width), bf), V((rows, width), bf),
+            V((2, cols, ff), f32), V((ff, cols), f32),
+            pltpu.SemaphoreType.DMA((4 + 3 * n_dp,)),
+            pltpu.SemaphoreType.DMA((4,)),
+            pltpu.SemaphoreType.DMA((n_remote,)),
+            pltpu.SemaphoreType.DMA((n_remote,)),
+        ],
+        compiler_params=pltpu.CompilerParams(
+            collective_id=0, has_side_effects=True, vmem_limit_bytes=56 * 1024 * 1024
+        ),
+    )(
+        section_lags, norm_gain, in_scales[0].reshape(4, cols), out_scales[0].reshape(2, cols),
+        xf, xb, dy, in_weight[0], out_weight[0], in_codes[0], out_codes[0],
+    )
+    return tuple(o[None] for o in outs)
+
+
 def solution(mesh):
     in_specs = (
         P("section", "dp", None),
@@ -155,4 +656,8 @@
         P("section", None, "dp", "hid"),
         P("section", "hid", "dp"),
     )
-    return jax.shard_map(local, mesh=mesh, in_specs=in_specs, out_specs=out_specs, check_vma=False)
+    if (mesh.shape["dp"], mesh.shape["hid"]) == (4, 2):
+        body = functools.partial(tick, mesh.shape["section"], mesh.shape["dp"])
+    else:
+        body = local
+    return jax.shard_map(body, mesh=mesh, in_specs=in_specs, out_specs=out_specs, check_vma=False)

time: 194 us -> 63.3 us (0.33)
  waiting for transfers between devices: 140 us -> 0 us
  Pallas kernels: 0 us -> 53.9 us
  other arithmetic: 15.4 us -> 0.03 us
  matrix products: 15.1 us -> 0 us
  between operations: 14.6 us -> 1.32 us
  starting transfers between devices: 5.21 us -> 0 us
  local copies, waits for them, and re-layouts: 3.42 us -> 7.75 us
    all_gather x2 -> x0, waiting for transfers between devices: 62.2 us -> none  [the longest x1 37.7 us: local(): lax.all_gather(pred_in, 'dp', axis=1, tiled=True)]
    pallas_call x0 -> x1, Pallas kernels: none -> 53.9 us  [tick(): pl.pallas_call(functools.partial(tick_kernel, n_sec), out_shape=(jax.Shap...]
    reduce_scatter x2 -> x0, waiting for transfers between devices: 39.7 us -> none  [the longest x1 28 us: local(): lax.psum_scatter(local_out.astype(jnp.bfloat16), 'dp', scatter_dimension=...]
    ppermute x2 -> x0, waiting for transfers between devices: 20 us -> none  [passed_along(): return lax.ppermute(block, axis, route)]
    psum x1 -> x0, waiting for transfers between devices: 17.8 us -> none  [local(): lax.psum(partial_value.astype(jnp.bfloat16), 'hid').astype(jnp.float32)]
    dot_general x10 -> x0, matrix products: 15.1 us -> none  [the longest x1 3.51 us: local(): jnp.dot(hidden, full_out, preferred_element_type=jnp.float32)]
    broadcast_in_dim x2 -> x0, other arithmetic: 6.92 us -> none  [local(): return (next_rows[None], back_rows[None], in_update[None], out_update[None])]
    convert_element_type x3 -> x0, other arithmetic: 6.15 us -> none  [the longest x1 4.11 us: local(): (in_weight[0] - LEARN_RATE * lag_value * direction(m_in, v_in, STEP - 1))...]
  transfers between devices with their start and end apart: 7 -> 0, of which waited for: 7 -> 0; matrix products, arithmetic and copies ran while one was open for 4% -> 0% of each run, Pallas kernels for 0% -> 0%
where the time goes in v1:
time: 63.3 us; the launch traced here: 63 us
  Pallas kernels  53.9 us (85%)
  local copies, waits for them, and re-layouts  7.75 us (12%)
  between operations  1.32 us (2%)
    pallas_call x1, Pallas kernels, tick(): pl.pallas_call(functools.partial(tick_kernel, n_sec), out_shape=(jax.Shap...  53.9 us
    unnamed x15, local copies, waits for them, and re-layouts  7.13 us

profile of v1, /device:TPU:0, one launch (start us, length us, event | category | flops | bytes accessed | tf_op | source)
XLA Modules:
  0.0 63.0 jit_solution(16513785595701554676)
XLA Ops:
  1.3 0.0 copy-start.4
  1.3 0.0 copy-start.3
  1.3 0.7 %copy-done.4 = f32[1,2,1,512]{3,2,1,0:T(1,128)S(1)} copy-done((f32[1,2,1,512]{3,2,1,0:T(1,128)S(1)}, f32[1,2,1,512]{3,2,1,0:T(1,128)}, u32[]{:S(2)}) %copy-start.4) | copy-done | bytes 4120
  2.0 0.6 copy.18
  2.6 0.0 copy-done.3
  2.6 0.6 reshape_squeeze.6.s_in_ref
  3.2 53.9 %shard_map.138 = (bf16[192,2048]{1,0:T(8,128)(2,1)}, bf16[192,2048]{1,0:T(8,128)(2,1)}, f32[2,512,256]{2,1,0:T(8,128)}, f32[256,512]{1,0:T(8,128)}) custom-call(s32[1]{0:T(128)S(6)} %copy.23.lag_ref, f32[1,2048]{1,0:T(1,128)} %gain_ref.1, f32[4,512]{1,0:T(4,128)} %reshape_squeeze.6.s_in_ref, f32[2,512]{1,0:T(2,128)} %bitcast.25, bf16[192,2048]{1,0:T(8,128)(2,1)} %bitcast.17, ...), custom_call_target="tpu_custom_call" | custom-call | tf_op jit(solution)/shard_map/pallas_call | solution.py:602
  57.1 0.0 copy-start.1
  57.1 2.2 %copy.24 = bf16[1,192,2048]{2,1,0:T(8,128)(2,1)} copy(bf16[1,192,2048]{2,1,0:T(8,128)(2,1)} %bitcast.21) | data formatting | bytes 1572864
  59.3 0.0 copy-done.1
  59.3 0.0 copy-start
  59.3 0.9 %copy.25 = bf16[1,192,2048]{2,1,0:T(8,128)(2,1)} copy(bf16[1,192,2048]{2,1,0:T(8,128)(2,1)S(1)} %bitcast.20) | data formatting | bytes 1572864
  60.2 0.6 copy-done
  60.8 0.0 copy-start.2
  60.8 1.0 %copy.26 = f32[1,2,512,256]{3,2,1,0:T(8,128)} copy(f32[1,2,512,256]{3,2,1,0:T(8,128)S(1)} %bitcast.16) | data formatting | bytes 2097152
  61.8 0.4 copy-done.2
  62.2 0.8 %copy.27 = f32[1,256,512]{2,1,0:T(8,128)} copy(f32[1,256,512]{2,1,0:T(8,128)S(1)} %bitcast.24) | data formatting | bytes 1048576
  (1 shorter events, 0.0 us)
Async XLA Ops:
  1.3 0.7 %copy-start.4 = (f32[1,2,1,512]{3,2,1,0:T(1,128)S(1)}, f32[1,2,1,512]{3,2,1,0:T(1,128)}, u32[]{:S(2)}) copy-start(f32[1,2,1,512]{3,2,1,0:T(1,128)} %param.20) | copy-start | bytes 12292
  1.3 1.3 %copy-start.3 = (f32[1,2,2,512,1]{3,4,2,1,0:T(1,128)S(1)}, f32[1,2,2,512,1]{3,4,2,1,0:T(1,128)}, u32[]{:S(2)}) copy-start(f32[1,2,2,512,1]{3,4,2,1,0:T(1,128)} %param.19) | copy-start | bytes 24580
  57.1 2.2 %copy-start.1 = (bf16[192,2048]{1,0:T(8,128)(2,1)S(1)}, bf16[192,2048]{1,0:T(8,128)(2,1)}, u32[]{:S(2)}) copy-start(bf16[192,2048]{1,0:T(8,128)(2,1)} %get-tuple-element.9) | copy-start | bytes 2359300
  59.3 1.5 %copy-start = (f32[2,512,256]{2,1,0:T(8,128)S(1)}, f32[2,512,256]{2,1,0:T(8,128)}, u32[]{:S(2)}) copy-start(f32[2,512,256]{2,1,0:T(8,128)} %get-tuple-element.10) | copy-start | bytes 3145732
  60.8 1.4 %copy-start.2 = (f32[256,512]{1,0:T(8,128)S(1)}, f32[256,512]{1,0:T(8,128)}, u32[]{:S(2)}) copy-start(f32[256,512]{1,0:T(8,128)} %get-tuple-element.11) | copy-start | bytes 1572868

commit v2 on v1

--- a/solution.py
+++ b/solution.py
@@ -170,23 +170,29 @@
     return (weight - top / bottom).astype(jnp.bfloat16)
 
 
-def updated(grad, codes, first_scale, second_scale):
+def decayed(codes, first_scale, second_scale):
     moment_m, root_v = moments(codes, first_scale, second_scale)
-    new_m = BETA_ONE * moment_m + (1.0 - BETA_ONE) * grad
-    new_v = BETA_TWO * (root_v * root_v) + (1.0 - BETA_TWO) * grad * grad
-    bottom = jnp.sqrt(new_v * (1.0 / (1.0 - BETA_TWO**STEP))) + ADAM_EPS
-    return new_m * (1.0 / (1.0 - BETA_ONE**STEP)) / bottom
+    keep_m = moment_m * (BETA_ONE / (1.0 - BETA_ONE**STEP))
+    keep_v = root_v * root_v * (BETA_TWO / (1.0 - BETA_TWO**STEP))
+    return keep_m, keep_v
+
+
+def updated(total, keep_m, keep_v, tokens):
+    part_m = (1.0 - BETA_ONE) / (1.0 - BETA_ONE**STEP) / tokens
+    part_v = (1.0 - BETA_TWO) / (1.0 - BETA_TWO**STEP) / tokens**2
+    new_v = keep_v + part_v * (total * total)
+    return (keep_m + part_m * total) / (jnp.sqrt(new_v) + ADAM_EPS)
 
 
 def tick_kernel(
     n_sec,
     lag_ref, gain_ref, s_in_ref, s_out_ref,
     xf_hbm, xb_hbm, dy_hbm, w_in_hbm, w_out_hbm, c_in_hbm, c_out_hbm,
-    y_out, dx_out, u_in_out, u_out_out,
+    y_b, dx_b, g_out, g_in, m_in, v_in,
     xf, xb, dy, w_in, w_out, c_in, c_out, s_t,
     p_in, p_out, nrm, acc, dh, hid, dgdu, h_all, n_all, dy_all,
-    q_s, q_r, e_s, e_r, y_s, dx_s, y_b, dx_b, g_in, g_out,
-    load_sem, store_sem, send_sem, recv_sem,
+    q_s, q_r, e_s, e_r, y_s, dx_s,
+    load_sem, send_sem, recv_sem,
 ):
     sec = lax.axis_index("section")
     me = lax.axis_index("dp")
@@ -222,7 +228,14 @@
     def load_cols(src, dst):
         return [load(src.at[:, pl.ds(j * cols, cols)], dst.at[j]) for j in range(n_dp)]
 
-    l_in = [load(c_in_hbm, c_in), load(w_in_hbm, w_in)]
+    half_c = cols // 2
+    l_in = [
+        [
+            load(src.at[:, pl.ds(at, half_c)], dst.at[:, pl.ds(at, half_c)])
+            for src, dst in ((c_in_hbm, c_in), (w_in_hbm, w_in))
+        ]
+        for at in (0, half_c)
+    ]
     l_out = [load(c_out_hbm, c_out), load(w_out_hbm, w_out)]
     l_xb = load_cols(xb_hbm, xb)
     l_xf = load_cols(xf_hbm, xf)
@@ -241,15 +254,10 @@
         pl.semaphore_signal(barrier, inc=1, device_id=below, device_id_type=MESH)
 
     step = LEARN_RATE * lag_ref[0].astype(jnp.float32)
-    for i in range(4):
-        s_t[i] = jnp.transpose(jnp.broadcast_to(s_in_ref[i : i + 1, :], (128, cols)))
     reps = ff // 128
 
     def row_scale(i, at):
         return jnp.concatenate([s_t[i, at, :]] * reps, axis=1)
-
-    for c in l_in:
-        c.wait()
 
     def predict_in(start):
         @pl.loop(0, cols // 2 // 32)
@@ -278,18 +286,48 @@
     h_x, h_y, h_on_y, h_on_x = spread(h_all, rlo, rhi)
     g_x, g_y, g_on_y, g_on_x = spread(dgdu, rlo, rhi)
 
-    predict_in(0)
+    mine = pl.ds(pl.multiple_of(core * half_r, half_r), half_r)
+    mine_b = pl.ds(pl.multiple_of(rows + core * half_r, half_r), half_r)
+    peers = ((1, me_x, dev_x), (2, me_y, dev_y), (3, me_d, dev_d))
+
+    def columns(owner):
+        return pl.ds(pl.multiple_of(owner * cols, cols), cols)
+
+    share = [
+        (
+            remote(dy_hbm.at[mine, columns(owner)], dy_all.at[slot, mine], dev),
+            remote(dy_all.at[slot, mine], dy_all.at[slot, mine], sibling),
+        )
+        for slot, owner, dev in peers
+    ]
+    share += [
+        (
+            remote(nrm.at[owner, mine_b], n_all.at[slot, mine], dev),
+            remote(n_all.at[slot, mine], n_all.at[slot, mine], sibling),
+        )
+        for slot, owner, dev in peers
+    ]
+
     expect = 4 + jnp.where(sec > 0, 1, 0) + jnp.where(sec < n_sec - 1, 1, 0)
     pl.semaphore_wait(barrier, expect)
+    for c, _ in share[:3]:
+        c.start()
+    for i in range(4):
+        s_t[i] = jnp.transpose(jnp.broadcast_to(s_in_ref[i], (128, cols)))
+    for c in l_in[0]:
+        c.wait()
+    predict_in(0)
     a_x[0].start()
     a_y[0].start()
+    for c in l_in[1]:
+        c.wait()
     predict_in(hc)
     a_y[1].start()
     a_x[1].start()
 
     for c in l_out:
         c.wait()
-    sm, sv = s_out_ref[0:1, :], s_out_ref[1:2, :]
+    sm, sv = s_out_ref[0], s_out_ref[1]
 
     @pl.loop(0, ff // 32)
     def _(t):
@@ -330,6 +368,15 @@
     n_all[0] = nrm[me, rows:, :]
     dy_all[0] = dy[me]
 
+    @pl.loop(0, cols // 32)
+    def _(t):
+        at = pl.ds(pl.multiple_of(t * 32, 32), 32)
+        for k in range(2):
+            lanes = slice(k * ff, (k + 1) * ff)
+            m_in[at, lanes], v_in[at, lanes] = decayed(
+                c_in[k, at, :], row_scale(k, at), row_scale(2 + k, at)
+            )
+
     a_x[0].wait_recv()
     a_on_y.start()
     a_y[1].wait_recv()
@@ -343,19 +390,7 @@
     d_y[1].wait_recv()
     d_on_x.start()
 
-    mine = pl.ds(pl.multiple_of(core * half_r, half_r), half_r)
-    mine_b = pl.ds(pl.multiple_of(rows + core * half_r, half_r), half_r)
-    share = []
-    for slot, owner, dev in ((1, me_x, dev_x), (2, me_y, dev_y), (3, me_d, dev_d)):
-        share.append((
-            remote(dy.at[owner, mine], dy_all.at[slot, mine], dev),
-            remote(dy_all.at[slot, mine], dy_all.at[slot, mine], sibling),
-        ))
-        share.append((
-            remote(nrm.at[owner, mine_b], n_all.at[slot, mine], dev),
-            remote(n_all.at[slot, mine], n_all.at[slot, mine], sibling),
-        ))
-    for c, _ in share:
+    for c, _ in share[3:]:
         c.start()
 
     d_x[1].wait_recv()
@@ -518,40 +553,21 @@
     h_on_y.wait_recv()
     h_on_x.wait_recv()
     tokens = n_dp * rows
-    share_of = 1.0 / tokens
     g_out[...] = matmul_tn(h_all[...].reshape(tokens, ff), dy_all[...].reshape(tokens, cols))
 
     @pl.loop(0, ff // 32)
     def _(t):
         at = pl.ds(pl.multiple_of(t * 32, 32), 32)
-        g_out[at, :] = updated(g_out[at, :] * share_of, c_out[at, :], sm, sv)
-
-    store_ids = iter(range(store_sem.shape[0]))
-
-    def store(src, dst):
-        copy = pltpu.make_async_copy(src, dst, store_sem.at[next(store_ids)])
-        copy.start()
-        return copy
-
-    stores = [store(g_out, u_out_out)]
+        keep_m, keep_v = decayed(c_out[at, :], sm, sv)
+        g_out[at, :] = updated(g_out[at, :], keep_m, keep_v, tokens)
 
     g_x[1].wait_recv()
     g_y[0].wait_recv()
+    near = 3 * rows
+    g_in[...] = matmul_tn(n_all[:3].reshape(near, cols), dgdu[:3].reshape(near, 2 * ff))
     g_on_y.wait_recv()
     g_on_x.wait_recv()
-    grad_in = matmul_tn(n_all[...].reshape(tokens, cols), dgdu[...].reshape(tokens, 2 * ff))
-    for k in range(2):
-        g_in[k] = grad_in[:, k * ff : (k + 1) * ff]
-
-    @pl.loop(0, cols // 32)
-    def _(t):
-        at = pl.ds(pl.multiple_of(t * 32, 32), 32)
-        for k in range(2):
-            g_in[k, at, :] = updated(
-                g_in[k, at, :] * share_of, c_in[k, at, :], row_scale(k, at), row_scale(2 + k, at)
-            )
-
-    stores.append(store(g_in, u_in_out))
+    g_in[...] += matmul_tn(n_all[3], dgdu[3])
 
     @pl.when(jnp.logical_not(first))
     def _():
@@ -569,8 +585,6 @@
         for c, _ in y_m:
             c.wait_send()
 
-    stores.append(store(y_b, y_out))
-    stores.append(store(dx_b, dx_out))
     for group in ((a_x, a_y, a_on_y, a_on_x), (d_x, d_y, d_on_y, d_on_x),
                   (h_x, h_y, h_on_y, h_on_x), (g_x, g_y, g_on_y, g_on_x)):
         for c in (*group[0], *group[1], group[2], group[3]):
@@ -580,7 +594,34 @@
         on.wait_send()
     for c in (*q_x, *e_x):
         c.wait_send()
-    for c in stores:
+
+
+def finish_kernel(
+    tokens, y_b, dx_b, u_out, g_in, m_in, v_in,
+    y_hbm, dx_hbm, u_in_hbm, u_out_hbm, u_in, sem,
+):
+    _, cols, ff = u_in.shape
+    copies = [
+        pltpu.make_async_copy(src, dst, sem.at[i])
+        for i, (src, dst) in enumerate(((y_b, y_hbm), (dx_b, dx_hbm), (u_out, u_out_hbm)))
+    ]
+    for c in copies:
+        c.start()
+    pieces = 2
+    tall = cols // pieces
+    for piece in range(pieces):
+        @pl.loop(0, tall // 32)
+        def _(t, piece=piece):
+            at = pl.ds(pl.multiple_of(piece * tall + t * 32, 32), 32)
+            for k in range(2):
+                lanes = slice(k * ff, (k + 1) * ff)
+                u_in[k, at, :] = updated(g_in[at, lanes], m_in[at, lanes], v_in[at, lanes], tokens)
+
+        at = pl.ds(piece * tall, tall)
+        c = pltpu.make_async_copy(u_in.at[:, at], u_in_hbm.at[:, at], sem.at[3 + piece])
+        c.start()
+        copies.append(c)
+    for c in copies:
         c.wait()
 
 
@@ -595,20 +636,22 @@
     half_r = rows // 2
     bf, f32 = jnp.bfloat16, jnp.float32
     vmem = pl.BlockSpec(memory_space=pltpu.VMEM)
-    hbm = pl.BlockSpec(memory_space=pl.ANY)
+    hbm = pl.BlockSpec(memory_space=pltpu.HBM)
     V = pltpu.VMEM
     wide = (n_dp, rows, cols)
     n_remote = 4 * 6 + 12 + 2 * CHUNKS + 4 * CHUNKS
-    outs = pl.pallas_call(
+    held = pl.pallas_call(
         functools.partial(tick_kernel, n_sec),
         out_shape=(
-            jax.ShapeDtypeStruct((rows, width), bf),
-            jax.ShapeDtypeStruct((rows, width), bf),
-            jax.ShapeDtypeStruct((2, cols, ff), f32),
-            jax.ShapeDtypeStruct((ff, cols), f32),
+            V((rows, width), bf),
+            V((rows, width), bf),
+            V((ff, cols), f32),
+            V((cols, 2 * ff), f32),
+            V((cols, 2 * ff), f32),
+            V((cols, 2 * ff), f32),
         ),
         in_specs=[pl.BlockSpec(memory_space=pltpu.SMEM), vmem, vmem, vmem] + [hbm] * 7,
-        out_specs=(hbm,) * 4,
+        out_specs=(vmem,) * 6,
         scratch_shapes=[
             V(wide, bf), V(wide, bf), V(wide, bf),
             V((2, cols, ff), f32), V((ff, cols), f32),
@@ -619,20 +662,31 @@
             V((2 * rows, 2 * ff), f32), V((rows, ff), f32), V((rows, ff), bf),
             V((n_dp, rows, 2 * ff), bf), V((n_dp, rows, ff), bf), V(wide, bf), V(wide, bf),
             V(wide, bf), V((n_dp, half_r, cols), bf), V(wide, bf), V((n_dp, half_r, cols), bf),
-            V((half_r, width), bf), V((half_r, width), bf), V((rows, width), bf), V((rows, width), bf),
-            V((2, cols, ff), f32), V((ff, cols), f32),
-            pltpu.SemaphoreType.DMA((4 + 3 * n_dp,)),
-            pltpu.SemaphoreType.DMA((4,)),
+            V((half_r, width), bf), V((half_r, width), bf),
+            pltpu.SemaphoreType.DMA((6 + 3 * n_dp,)),
             pltpu.SemaphoreType.DMA((n_remote,)),
             pltpu.SemaphoreType.DMA((n_remote,)),
         ],
         compiler_params=pltpu.CompilerParams(
-            collective_id=0, has_side_effects=True, vmem_limit_bytes=56 * 1024 * 1024
+            collective_id=0, has_side_effects=True, vmem_limit_bytes=61200000
         ),
     )(
-        section_lags, norm_gain, in_scales[0].reshape(4, cols), out_scales[0].reshape(2, cols),
+        section_lags, norm_gain, jnp.swapaxes(in_scales[0], 2, 3).reshape(4, 1, cols), out_scales[0],
         xf, xb, dy, in_weight[0], out_weight[0], in_codes[0], out_codes[0],
     )
+    outs = pl.pallas_call(
+        functools.partial(finish_kernel, rows * n_dp),
+        out_shape=(
+            jax.ShapeDtypeStruct((rows, width), bf),
+            jax.ShapeDtypeStruct((rows, width), bf),
+            jax.ShapeDtypeStruct((2, cols, ff), f32),
+            jax.ShapeDtypeStruct((ff, cols), f32),
+        ),
+        in_specs=[vmem] * 6,
+        out_specs=(hbm,) * 4,
+        scratch_shapes=[V((2, cols, ff), f32), pltpu.SemaphoreType.DMA((5,))],
+        compiler_params=pltpu.CompilerParams(vmem_limit_bytes=16 * 1024 * 1024),
+    )(*held)
     return tuple(o[None] for o in outs)
 
 

time: 63.3 us -> 55.8 us (0.88)
  local copies, waits for them, and re-layouts: 7.75 us -> 0 us
    unnamed x15 -> x0, local copies, waits for them, and re-layouts: 7.13 us -> none
    pallas_call x1 -> x2, Pallas kernels: 53.9 us -> 54.3 us  [the longest x1 52.6 us: tick(): pl.pallas_call(functools.partial(tick_kernel, n_sec), out_shape=(V((rows,...]
where the time goes in v2:
time: 55.8 us; the launch traced here: 55.6 us
  Pallas kernels  54.3 us (97%)
  between operations  1.29 us (2%)
    pallas_call x1, Pallas kernels, tick(): pl.pallas_call(functools.partial(tick_kernel, n_sec), out_shape=(V((rows,...  52.6 us
    pallas_call x1, Pallas kernels, tick(): pl.pallas_call(functools.partial(finish_kernel, rows * n_dp), out_shape=(...  1.7 us

profile of v2, /device:TPU:0, one launch (start us, length us, event | category | flops | bytes accessed | tf_op | source)
XLA Modules:
  0.0 55.6 jit_solution(9135965053723223527)
XLA Ops:
  1.3 52.6 %shard_map.138 = (bf16[192,2048]{1,0:T(8,128)(2,1)S(1)}, bf16[192,2048]{1,0:T(8,128)(2,1)S(1)}, f32[256,512]{1,0:T(8,128)S(1)}, f32[512,512]{1,0:T(8,128)S(1)}, ...) custom-call(s32[1]{0:T(128)S(6)} %copy.15.lag_ref, f32[1,2048]{1,0:T(1,128)} %gain_ref.1, f32[4,1,512]{2,1,0:T(1,128)} %bitcast.20, ...), custom_call_target="tpu_custom_call" | custom-call | tf_op jit(solution)/shard_map/pallas_call | solution.py:643
  53.9 1.7 %shard_map.139 = (bf16[192,2048]{1,0:T(8,128)(2,1)}, bf16[192,2048]{1,0:T(8,128)(2,1)}, f32[2,512,256]{2,1,0:T(8,128)}, f32[256,512]{1,0:T(8,128)}) custom-call(bf16[192,2048]{1,0:T(8,128)(2,1)S(1)} %get-tuple-element.14.y_b, bf16[192,2048]{1,0:T(8,128)(2,1)S(1)} %get-tuple-element.15.dx_b, f32[256,512]{1,0:T(8,128)S(1)} %get-tuple-element.16.u_out, ...), custom_call_target="tpu_custom_call" | custom-call | tf_op jit(solution)/shard_map/pallas_call | solution.py:677

commit v3 on v2

--- a/solution.py
+++ b/solution.py
@@ -310,8 +310,6 @@
 
     expect = 4 + jnp.where(sec > 0, 1, 0) + jnp.where(sec < n_sec - 1, 1, 0)
     pl.semaphore_wait(barrier, expect)
-    for c, _ in share[:3]:
-        c.start()
     for i in range(4):
         s_t[i] = jnp.transpose(jnp.broadcast_to(s_in_ref[i], (128, cols)))
     for c in l_in[0]:
@@ -390,6 +388,8 @@
     d_y[1].wait_recv()
     d_on_x.start()
 
+    for c, _ in share[:3]:
+        c.start()
     for c, _ in share[3:]:
         c.start()
 

time: 55.8 us -> 54.7 us (0.980)
  Pallas kernels: 54.3 us -> 53.2 us
    pallas_call x1, Pallas kernels: 52.6 us -> 51.5 us  [tick(): pl.pallas_call(functools.partial(tick_kernel, n_sec), out_shape=(V((rows,...]
where the time goes in v3:
time: 54.7 us; the launch traced here: 54.4 us
  Pallas kernels  53.2 us (97%)
  between operations  1.29 us (2%)
    pallas_call x1, Pallas kernels, tick(): pl.pallas_call(functools.partial(tick_kernel, n_sec), out_shape=(V((rows,...  51.5 us
    pallas_call x1, Pallas kernels, tick(): pl.pallas_call(functools.partial(finish_kernel, rows * n_dp), out_shape=(...  1.7 us

profile of v3, /device:TPU:0, one launch (start us, length us, event | category | flops | bytes accessed | tf_op | source)
XLA Modules:
  0.0 54.4 jit_solution(7295850605961538)
XLA Ops:
  1.3 51.5 %shard_map.138 = (bf16[192,2048]{1,0:T(8,128)(2,1)S(1)}, bf16[192,2048]{1,0:T(8,128)(2,1)S(1)}, f32[256,512]{1,0:T(8,128)S(1)}, f32[512,512]{1,0:T(8,128)S(1)}, ...) custom-call(s32[1]{0:T(128)S(6)} %copy.15.lag_ref, f32[1,2048]{1,0:T(1,128)} %gain_ref.1, f32[4,1,512]{2,1,0:T(1,128)} %bitcast.20, ...), custom_call_target="tpu_custom_call" | custom-call | tf_op jit(solution)/shard_map/pallas_call | solution.py:643
  52.7 1.7 %shard_map.139 = (bf16[192,2048]{1,0:T(8,128)(2,1)}, bf16[192,2048]{1,0:T(8,128)(2,1)}, f32[2,512,256]{2,1,0:T(8,128)}, f32[256,512]{1,0:T(8,128)}) custom-call(bf16[192,2048]{1,0:T(8,128)(2,1)S(1)} %get-tuple-element.14.y_b, bf16[192,2048]{1,0:T(8,128)(2,1)S(1)} %get-tuple-element.15.dx_b, f32[256,512]{1,0:T(8,128)S(1)} %get-tuple-element.16.u_out, ...), custom_call_target="tpu_custom_call" | custom-call | tf_op jit(solution)/shard_map/pallas_call | solution.py:677
